TPU v7x, 128 devices: a whole 4x4x4 slice. The times are simulated.
128 devices in a mesh: gx: 16 (over z, y), gy: 8 (over x, core).
Axes of the slice: x: 4, y: 4, z: 4, core: 2. Of those that a mesh axis runs over, the one named last changes fastest.
Arguments:
- pumping: float32 [16, 4, 128, 1024], P(None, None, 'gx', 'gy'), may hold values from -1080 to 1080
- conductivity: float32 [4, 128, 1024], P(None, 'gx', 'gy'), may hold values from 0.2 to 5
- capacity: float32 [4, 128, 1024], P(None, 'gx', 'gy'), may hold values from 1 to 10
Outputs:
- solution: float32 [16, 4, 128, 1024], P(None, None, 'gx', 'gy')
- residual: float32 [16, 4, 128, 1024], P(None, None, 'gx', 'gy')
All inputs are finite; a program needn't handle non-finite values.
Results may differ from a plain program's by a relative error of at most 0.0035.
Values sent between devices are 32-bit elements; how exact they have to be, the bound alone decides.
A program may use at most 64 MiB of HBM per device.

v0:
```python
import jax
import jax.numpy as jnp
from jax import lax
from jax.sharding import PartitionSpec as P

RHS = 16
S = 4
CYCLES = 5
BASIS = 80


def padded_2(array, sides, width):
    for axis, dim in sides:
        devices, length = (lax.axis_size(axis), array.shape[dim])
        up = [(i, (i + 1) % devices) for i in range(devices - 1)]
        down = [(j, i) for i, j in up]
        last = lax.slice_in_dim(array, length - width, length, axis=dim)
        leading = lax.slice_in_dim(array, 0, width, axis=dim)
        before = lax.ppermute(last, axis, up)
        after = lax.ppermute(leading, axis, down)
        array = jnp.concatenate([before, array, after], axis=dim)
    return array


def face_terms(padded, storage):
    core = padded[1:-1, 1:-1, 1:-1]
    terms = (
        (core + padded[:-2, 1:-1, 1:-1]) * 0.5,
        (core + padded[2:, 1:-1, 1:-1]) * 0.5,
        (core + padded[1:-1, :-2, 1:-1]) * 0.5,
        (core + padded[1:-1, 2:, 1:-1]) * 0.5,
        (core + padded[1:-1, 1:-1, :-2]) * 0.5,
        (core + padded[1:-1, 1:-1, 2:]) * 0.5,
    )
    diagonal = storage + terms[0] + terms[1] + terms[2] + terms[3] + terms[4] + terms[5]
    return (terms, diagonal)


def apply_off(padded, terms):
    total = terms[0] * padded[:, :-2, 1:-1, 1:-1] + terms[1] * padded[:, 2:, 1:-1, 1:-1]
    total = total + terms[2] * padded[:, 1:-1, :-2, 1:-1] + terms[3] * padded[:, 1:-1, 2:, 1:-1]
    total = total + terms[4] * padded[:, 1:-1, 1:-1, :-2] + terms[5] * padded[:, 1:-1, 1:-1, 2:]
    return total


def small_solve(gram_all):
    shift_matrix = jnp.eye(BASIS, BASIS - RHS, dtype=jnp.float32) + jnp.eye(
        BASIS, BASIS - RHS, k=-RHS, dtype=jnp.float32
    )
    first_block = jnp.eye(BASIS, RHS, dtype=jnp.float32)
    hp = lax.Precision.HIGHEST
    gram_shift = jnp.dot(gram_all, shift_matrix, precision=hp)
    normal = jnp.dot(shift_matrix.T, gram_shift, precision=hp)
    right_side = jnp.dot(gram_shift.T, first_block, precision=hp)
    lower = jnp.linalg.cholesky(normal)
    y = jax.scipy.linalg.cho_solve((lower, True), right_side)
    coeffs = first_block - jnp.dot(shift_matrix, y, precision=hp)
    return (y, coeffs)


def shards(pumping, conductivity, capacity):
    hp = lax.Precision.HIGHEST
    shape = pumping.shape
    cond_halo = padded_2(conductivity, (("gx", 1), ("gy", 2)), 1)
    cond_pad = jnp.pad(cond_halo, ((1, 1), (0, 0), (0, 0)))
    terms, diagonal = face_terms(cond_pad, capacity)
    solution = jnp.zeros(shape, jnp.float32)
    residual = pumping / diagonal
    for restart in range(CYCLES):
        blocks = [residual]
        for k in range(S):
            bordered = padded_2(blocks[-1], (("gx", 2), ("gy", 3)), 1)
            padded = jnp.pad(bordered, ((0, 0), (1, 1), (0, 0), (0, 0)))
            blocks.append(-apply_off(padded, terms) / diagonal)
        stacked = jnp.concatenate(blocks, 0).reshape(BASIS, -1)
        local_gram = jnp.dot(stacked, stacked.T, precision=hp)
        gram_all = lax.psum(local_gram, ("gx", "gy"))
        y, coeffs = small_solve(gram_all)
        solution = solution + jnp.dot(y.T, stacked[: BASIS - RHS], precision=hp).reshape(shape)
        residual = jnp.dot(coeffs.T, stacked, precision=hp).reshape(shape)
    return (solution, residual)


def solution(mesh):
    return jax.shard_map(
        shards,
        mesh=mesh,
        in_specs=(P(None, None, "gx", "gy"), P(None, "gx", "gy"), P(None, "gx", "gy")),
        out_specs=(P(None, None, "gx", "gy"), P(None, None, "gx", "gy")),
        check_vma=False,
    )
```

profile of v0, /device:TPU:1, one launch (start us, length us, event | category | flops | bytes accessed | tf_op | source)
XLA Modules:
  0.0 885.2 jit_solution(18000092713170605420)
XLA Ops:
  1.4 4.0 collective-permute-start
  10.6 5.1 collective-permute-start.2
  39.3 4.4 collective-permute-done.7
  44.5 4.6 collective-permute-start.8
  61.1 4.4 collective-permute-done.11
  66.3 3.7 collective-permute-start.12
  82.1 4.4 collective-permute-done.15
  103.1 4.4 collective-permute-done.19
  109.9 68.0 %psum.35 = f32[80,80]{1,0:T(8,128)S(1)} all-reduce(f32[80,80]{1,0:T(8,128)S(1)} %convolution_bitcast_fusion.4), channel_id=1, replica_groups=mesh['gx'=16,'gy'=8] {'gx','gy'}, use_global_device_ids=true, to_apply=%region_0.1 | all-reduce | flops 6400 | bytes 51200 | tf_op jit(solution)/shard_map/psum | solution.py:77
  179.8 5.8 cholesky.89
  187.0 4.9 custom-call.11
  201.0 4.9 collective-permute-start.22
  210.0 4.4 collective-permute-done.23
  230.1 4.4 collective-permute-done.27
  235.3 4.8 collective-permute-start.28
  252.4 4.4 collective-permute-done.31
  273.4 4.4 collective-permute-done.35
  280.8 66.5 %psum.36 = f32[80,80]{1,0:T(8,128)} all-reduce(f32[80,80]{1,0:T(8,128)} %convolution_bitcast_fusion.3), channel_id=1, replica_groups=mesh['gx'=16,'gy'=8] {'gx','gy'}, use_global_device_ids=true, to_apply=%region_3.6 | all-reduce | flops 6400 | bytes 51200 | tf_op jit(solution)/shard_map/psum | solution.py:77
  352.3 5.8 cholesky.100
  359.5 4.9 custom-call.12
  374.5 4.3 collective-permute-start.38
  382.9 4.4 collective-permute-done.39
  403.0 4.4 collective-permute-done.43
  408.2 5.4 collective-permute-start.44
  425.6 4.4 collective-permute-done.47
  446.6 4.4 collective-permute-done.51
  454.5 66.5 %psum.37 = f32[80,80]{1,0:T(8,128)S(1)} all-reduce(f32[80,80]{1,0:T(8,128)S(1)} %convolution_bitcast_fusion.2), channel_id=1, replica_groups=mesh['gx'=16,'gy'=8] {'gx','gy'}, use_global_device_ids=true, to_apply=%region_4.7 | all-reduce | flops 6400 | bytes 51200 | tf_op jit(solution)/shard_map/psum | solution.py:77
  525.3 5.8 cholesky.111
  532.4 4.9 custom-call.13
  547.1 4.8 collective-permute-start.54
  555.9 4.4 collective-permute-done.55
  575.9 4.4 collective-permute-done.59
  581.1 4.7 collective-permute-start.60
  597.8 4.4 collective-permute-done.63
  619.3 3.9 collective-permute-done.67
  626.7 66.7 %psum.38 = f32[80,80]{1,0:T(8,128)S(1)} all-reduce(f32[80,80]{1,0:T(8,128)S(1)} %convolution_bitcast_fusion.1), channel_id=1, replica_groups=mesh['gx'=16,'gy'=8] {'gx','gy'}, use_global_device_ids=true, to_apply=%region_5.8 | all-reduce | flops 6400 | bytes 51200 | tf_op jit(solution)/shard_map/psum | solution.py:77
  697.7 5.8 cholesky.122
  704.9 4.9 custom-call.14
  719.4 5.7 collective-permute-start.70
  729.1 4.4 collective-permute-done.71
  748.7 4.4 collective-permute-done.75
  753.9 5.0 collective-permute-start.76
  771.0 4.4 collective-permute-done.79
  776.2 4.5 collective-permute-start.80
  792.7 4.4 collective-permute-done.83
  799.5 66.5 %psum.39 = f32[80,80]{1,0:T(8,128)S(1)} all-reduce(f32[80,80]{1,0:T(8,128)S(1)} %convolution_bitcast_fusion), channel_id=1, replica_groups=mesh['gx'=16,'gy'=8] {'gx','gy'}, use_global_device_ids=true, to_apply=%region_6.9 | all-reduce | flops 6400 | bytes 51200 | tf_op jit(solution)/shard_map/psum | solution.py:77
  867.9 5.8 cholesky.133
  875.1 4.9 custom-call.15
  (373 shorter events, 345.4 us)
Async XLA Ops:
  1.4 5.3 collective-permute-start
  10.6 7.0 collective-permute-start.2
  32.0 7.3 collective-permute-start.6
  35.3 8.4 collective-permute-start.7
  44.5 5.9 collective-permute-start.8
  54.2 6.9 collective-permute-start.10
  57.1 8.4 collective-permute-start.11
  75.2 6.9 collective-permute-start.14
  78.1 8.4 collective-permute-start.15
  96.2 6.9 collective-permute-start.18
  99.1 8.4 collective-permute-start.19
  201.0 8.9 %collective-permute-start.22 = (f32[16,4,10,1]{3,0,2,1:T(8,128)S(1)}, f32[16,4,10,1]{3,0,2,1:T(8,128)S(1)}, u32[]{:S(2)}, u32[]{:S(2)}) collective-permute-start(f32[16,4,10,1]{3,0,2,1:T(8,128)S(1)} %get-tuple-element.77), channel_id=1, source_target_pairs={{0,1},{1,2},{2,3},{3,4},{4,5},{5,6},{6,7},{8,9},{9,10},{10,11},{11... | collective-permute-start | bytes 7688 | tf_op jit(solution)/shard_map/ppermute | solution.py:19
  206.0 8.4 collective-permute-start.23
  222.8 7.3 collective-permute-start.26
  226.1 8.4 collective-permute-start.27
  235.3 6.1 collective-permute-start.28
  245.2 7.2 collective-permute-start.30
  248.4 8.4 collective-permute-start.31
  266.2 7.2 collective-permute-start.34
  269.4 8.4 collective-permute-start.35
  374.5 8.4 collective-permute-start.38
  378.9 8.4 collective-permute-start.39
  396.1 6.9 collective-permute-start.42
  399.0 8.4 collective-permute-start.43
  408.2 6.7 collective-permute-start.44
  418.5 7.2 collective-permute-start.46
  421.6 8.4 collective-permute-start.47
  439.7 6.9 collective-permute-start.50
  442.6 8.4 collective-permute-start.51
  547.1 8.8 collective-permute-start.54
  551.9 8.4 collective-permute-start.55
  568.8 7.1 collective-permute-start.58
  571.9 8.4 collective-permute-start.59
  581.1 6.0 collective-permute-start.60
  590.9 6.9 collective-permute-start.62
  593.8 8.4 collective-permute-start.63
  611.9 7.4 collective-permute-start.66
  614.8 8.4 collective-permute-start.67
  719.4 9.7 %collective-permute-start.70 = (f32[16,4,10,1]{3,0,2,1:T(8,128)S(1)}, f32[16,4,10,1]{3,0,2,1:T(8,128)S(1)}, u32[]{:S(2)}, u32[]{:S(2)}) collective-permute-start(f32[16,4,10,1]{3,0,2,1:T(8,128)S(1)} %get-tuple-element.53), channel_id=1, source_target_pairs={{0,1},{1,2},{2,3},{3,4},{4,5},{5,6},{6,7},{8,9},{9,10},{10,11},{11... | collective-permute-start | bytes 7688 | tf_op jit(solution)/shard_map/ppermute | solution.py:19
  725.1 8.4 collective-permute-start.71
  741.5 7.2 collective-permute-start.74
  744.7 8.4 collective-permute-start.75
  753.9 7.6 collective-permute-start.76
  764.1 6.9 collective-permute-start.78
  767.0 8.4 collective-permute-start.79
  776.2 7.2 collective-permute-start.80
  785.8 6.9 collective-permute-start.82
  788.7 8.4 collective-permute-start.83
  (48 other events, 613.6 us)
where the time goes:
time: 894 us; the launch traced here: 885 us
  blocking collectives  334 us (37%)
  starting transfers between devices  214 us (24%)
  waiting for transfers between devices  190 us (21%)
  other arithmetic  80.5 us (9%)
  matrix products  34 us (4%)
  local copies, waits for them, and re-layouts  30.1 us (3%)
    psum x5, blocking collectives, shards(): gram_all = lax.psum(local_gram, ('gx', 'gy'))  334 us
    ppermute x42, waiting for transfers between devices, padded_2(): after = lax.ppermute(leading, axis, down)  157 us
    ppermute x42, starting transfers between devices, padded_2(): before = lax.ppermute(last, axis, up)  145 us
    ppermute x42, starting transfers between devices, padded_2(): after = lax.ppermute(leading, axis, down)  68.6 us
    another operation x15, other arithmetic, small_solve(): lower = jnp.linalg.cholesky(normal)  32.6 us
    ppermute x42, waiting for transfers between devices, padded_2(): before = lax.ppermute(last, axis, up)  32.5 us
    another operation x10, other arithmetic, small_solve(): y = jax.scipy.linalg.cho_solve((lower, True), right_side)  27.7 us
    unnamed x46, local copies, waits for them, and re-layouts  18.2 us
  transfers between devices with their start and end apart: 84, of which 61 were waited for; matrix products, arithmetic and copies ran while one was open for 2% of the time, Pallas kernels for 0%

commit v1 on v0

--- a/solution.py
+++ b/solution.py
@@ -74,7 +74,7 @@
             blocks.append(-apply_off(padded, terms) / diagonal)
         stacked = jnp.concatenate(blocks, 0).reshape(BASIS, -1)
         local_gram = jnp.dot(stacked, stacked.T, precision=hp)
-        gram_all = lax.psum(local_gram, ("gx", "gy"))
+        gram_all = jnp.sum(lax.all_gather(local_gram, ("gx", "gy")), axis=0)
         y, coeffs = small_solve(gram_all)
         solution = solution + jnp.dot(y.T, stacked[: BASIS - RHS], precision=hp).reshape(shape)
         residual = jnp.dot(coeffs.T, stacked, precision=hp).reshape(shape)

time: 894 us -> 918 us (1.027)
  waiting for transfers between devices: 190 us -> 526 us
  blocking collectives: 334 us -> 0 us
  other arithmetic: 80.5 us -> 95.6 us
  between operations: 2.94 us -> 16.3 us
    psum x5 -> x0, blocking collectives: 334 us -> none  [shards(): gram_all = lax.psum(local_gram, ('gx', 'gy'))]
    all_gather x0 -> x5, waiting for transfers between devices: none -> 321 us  [shards(): gram_all = jnp.sum(lax.all_gather(local_gram, ('gx', 'gy')), axis=0)]
    reduce_sum x0 -> x5, other arithmetic: none -> 14.5 us  [shards(): gram_all = jnp.sum(lax.all_gather(local_gram, ('gx', 'gy')), axis=0)]
  transfers between devices with their start and end apart: 84 -> 89, of which waited for: 61 -> 67; matrix products, arithmetic and copies ran while one was open for 2% -> 3% of each run, Pallas kernels for 0% -> 0%
where the time goes in v1:
time: 918 us; the launch traced here: 910 us
  waiting for transfers between devices  526 us (57%)
  starting transfers between devices  209 us (23%)
  other arithmetic  95.6 us (10%)
  matrix products  35.4 us (4%)
  local copies, waits for them, and re-layouts  27.2 us (3%)
  between operations  16.3 us (2%)
    all_gather x5, waiting for transfers between devices, shards(): gram_all = jnp.sum(lax.all_gather(local_gram, ('gx', 'gy')), axis=0)  321 us
    ppermute x42, waiting for transfers between devices, padded_2(): after = lax.ppermute(leading, axis, down)  164 us
    ppermute x42, starting transfers between devices, padded_2(): before = lax.ppermute(last, axis, up)  140 us
    ppermute x42, starting transfers between devices, padded_2(): after = lax.ppermute(leading, axis, down)  67.6 us
    ppermute x42, waiting for transfers between devices, padded_2(): before = lax.ppermute(last, axis, up)  41.3 us
    another operation x15, other arithmetic, small_solve(): lower = jnp.linalg.cholesky(normal)  32.6 us
    another operation x10, other arithmetic, small_solve(): y = jax.scipy.linalg.cho_solve((lower, True), right_side)  27.4 us
  transfers between devices with their start and end apart: 89, of which 67 were waited for; matrix products, arithmetic and copies ran while one was open for 3% of the time, Pallas kernels for 0%

profile of v1, /device:TPU:1, one launch (start us, length us, event | category | flops | bytes accessed | tf_op | source)
XLA Modules:
  0.0 910.2 jit_solution(2982100690045587182)
XLA Ops:
  8.0 4.0 collective-permute-start
  17.2 5.1 collective-permute-start.2
  45.9 4.4 collective-permute-done.7
  51.1 4.6 collective-permute-start.8
  67.7 4.4 collective-permute-done.11
  88.7 4.4 collective-permute-done.15
  93.9 3.7 collective-permute-start.16
  109.7 4.4 collective-permute-done.19
  119.9 67.6 %all-gather.11.cloned.1.call-done = f32[10240,80]{1,0:T(8,128)} async-done(((f32[80,80]{1,0:T(8,128)}), f32[10240,80]{1,0:T(8,128)}) %all-gather.11.cloned.1.call-update) | async-done | bytes 3276816 | tf_op jit(solution)/shard_map/all_gather | solution.py:77
  191.3 5.8 cholesky.89
  198.4 4.9 custom-call.11
  213.4 3.9 collective-permute-start.22
  221.3 4.4 collective-permute-done.23
  241.6 4.4 collective-permute-done.27
  246.9 4.5 collective-permute-start.28
  263.4 4.4 collective-permute-done.31
  268.6 3.7 collective-permute-start.32
  284.3 4.4 collective-permute-done.35
  294.2 67.0 %all-gather.13.cloned.1.call-done = f32[10240,80]{1,0:T(8,128)} async-done(((f32[80,80]{1,0:T(8,128)}), f32[10240,80]{1,0:T(8,128)}) %all-gather.13.cloned.1.call-update) | async-done | bytes 3276816 | tf_op jit(solution)/shard_map/all_gather | solution.py:77
  365.0 5.8 cholesky.100
  372.1 4.9 custom-call.12
  387.1 3.9 collective-permute-start.38
  395.0 4.4 collective-permute-done.39
  415.3 4.4 collective-permute-done.43
  420.5 4.5 collective-permute-start.44
  437.1 4.4 collective-permute-done.47
  458.0 4.4 collective-permute-done.51
  467.9 67.0 %all-gather.15.cloned.1.call-done = f32[10240,80]{1,0:T(8,128)} async-done(((f32[80,80]{1,0:T(8,128)}), f32[10240,80]{1,0:T(8,128)}) %all-gather.15.cloned.1.call-update) | async-done | bytes 3276816 | tf_op jit(solution)/shard_map/all_gather | solution.py:77
  538.7 5.8 cholesky.111
  545.8 4.9 custom-call.13
  560.8 3.9 collective-permute-start.54
  568.7 4.4 collective-permute-done.55
  589.0 4.4 collective-permute-done.59
  594.2 4.5 collective-permute-start.60
  610.7 4.4 collective-permute-done.63
  631.7 4.4 collective-permute-done.67
  641.8 66.8 %all-gather.17.cloned.1.call-done = f32[10240,80]{1,0:T(8,128)} async-done(((f32[80,80]{1,0:T(8,128)}), f32[10240,80]{1,0:T(8,128)}) %all-gather.17.cloned.1.call-update) | async-done | bytes 3276816 | tf_op jit(solution)/shard_map/all_gather | solution.py:77
  712.4 5.8 cholesky.122
  719.5 4.9 custom-call.14
  734.8 3.9 collective-permute-start.70
  742.7 4.4 collective-permute-done.71
  763.1 4.4 collective-permute-done.75
  768.3 4.5 collective-permute-start.76
  784.8 4.4 collective-permute-done.79
  805.8 4.4 collective-permute-done.83
  830.3 52.3 %all-gather.19.cloned.1.call-done = f32[10240,80]{1,0:T(8,128)} async-done(((f32[80,80]{1,0:T(8,128)}), f32[10240,80]{1,0:T(8,128)}) %all-gather.19.cloned.1.call-update) | async-done | bytes 3276816 | tf_op jit(solution)/shard_map/all_gather | solution.py:77
  886.4 5.8 cholesky.133
  893.6 4.9 custom-call.15
  (416 shorter events, 376.9 us)
Async XLA Ops:
  7.2 180.4 %all-gather.11.cloned.1.call-start = ((), (), s32[]{:S(2)}) async-start(), calls=%async_computation | async-start | bytes 5283840 | tf_op jit(solution)/shard_map/all_gather | solution.py:77
  17.2 7.0 collective-permute-start.2
  38.5 7.3 collective-permute-start.6
  41.9 8.4 collective-permute-start.7
  51.1 5.9 collective-permute-start.8
  60.8 6.9 collective-permute-start.10
  63.7 8.4 collective-permute-start.11
  81.8 6.9 collective-permute-start.14
  84.7 8.4 collective-permute-start.15
  102.8 6.9 collective-permute-start.18
  105.7 8.4 collective-permute-start.19
  116.7 244.5 %all-gather.13.cloned.1.call-start = ((), (), s32[]{:S(2)}) async-start(), calls=%async_computation.1 | async-start | bytes 5283840 | tf_op jit(solution)/shard_map/all_gather | solution.py:77
  213.4 7.9 collective-permute-start.22
  217.3 8.4 collective-permute-start.23
  234.5 7.2 collective-permute-start.26
  237.6 8.4 collective-permute-start.27
  246.9 5.8 collective-permute-start.28
  256.5 6.9 collective-permute-start.30
  259.4 8.4 collective-permute-start.31
  277.4 6.9 collective-permute-start.34
  280.4 8.4 collective-permute-start.35
  291.3 243.6 %all-gather.15.cloned.1.call-start = ((), (), s32[]{:S(2)}) async-start(), calls=%async_computation.2 | async-start | bytes 5283840 | tf_op jit(solution)/shard_map/all_gather | solution.py:77
  387.1 7.9 collective-permute-start.38
  391.0 8.4 collective-permute-start.39
  408.2 7.2 collective-permute-start.42
  411.3 8.4 collective-permute-start.43
  430.2 6.9 collective-permute-start.46
  433.1 8.4 collective-permute-start.47
  451.1 6.9 collective-permute-start.50
  454.0 8.4 collective-permute-start.51
  465.0 243.6 %all-gather.17.cloned.1.call-start = ((), (), s32[]{:S(2)}) async-start(), calls=%async_computation.3 | async-start | bytes 5283840 | tf_op jit(solution)/shard_map/all_gather | solution.py:77
  560.8 7.9 collective-permute-start.54
  564.7 8.4 collective-permute-start.55
  581.8 7.2 collective-permute-start.58
  585.0 8.4 collective-permute-start.59
  603.8 6.9 collective-permute-start.62
  606.7 8.4 collective-permute-start.63
  624.8 6.9 collective-permute-start.66
  627.7 8.4 collective-permute-start.67
  638.7 243.9 %all-gather.19.cloned.1.call-start = ((), (), s32[]{:S(2)}) async-start(), calls=%async_computation.4 | async-start | bytes 5283840 | tf_op jit(solution)/shard_map/all_gather | solution.py:77
  734.8 7.9 collective-permute-start.70
  738.8 8.4 collective-permute-start.71
  755.9 7.2 collective-permute-start.74
  759.1 8.4 collective-permute-start.75
  777.9 6.9 collective-permute-start.78
  780.8 8.4 collective-permute-start.79
  798.9 6.9 collective-permute-start.82
  801.8 8.4 collective-permute-start.83
  (67 other events, 489.3 us)
Sparse Core Ops, SparseCore 0:
  116.8 70.6 all-gather.10
  291.5 69.7 all-gather.12
  465.1 69.7 all-gather.14
  638.8 69.7 all-gather.16
  812.9 69.6 all-gather.18
